TPU v7x, 32 devices: a whole 2x2x4 slice. The times are simulated.
32 devices in a mesh: bas: 8 (over y, x, core), aux: 4 (over z).
Axes of the slice: x: 2, y: 2, z: 4, core: 2. Of those that a mesh axis runs over, the one named last changes fastest.
Arguments:
- integrals: bfloat16 [4, 8192, 8192], P('aux', 'bas'), may hold values from -6 to 6
- screen: int32 [4, 64, 64], P('aux', 'bas'), may hold values from 0 to 1, as said below
- coefficients: bfloat16 [8192, 384], P('bas'), may hold values from -0.0625 to 0.0625
- weights: float32 [384], replicated, may hold values from -2 to 2
Outputs:
- exchange: bfloat16 [8192, 8192], P('aux', 'bas')
Inputs may be any that keep to these rules, and one draw needn't show every extreme that they name: `screen`: every block with equal row and column block index is 1; the share of ones differs from row block to row block.
All inputs are finite; a program needn't handle non-finite values.
Results may differ from a plain program's by a relative error of at most 0.018.
Values may be sent and summed in bfloat16 or wider, within the bound.
A program may use at most 128 MiB of HBM per device.

v0:
```python
import math
import jax
import jax.numpy as jnp
from jax import lax
from jax.sharding import PartitionSpec as P

NOCC = 384
BLOCK = 128
AUX_DEV = 1


def spread_2(block, axis, owner):
    block = jnp.where(lax.axis_index(axis) == owner, block, jnp.zeros_like(block))
    return lax.psum(block, axis)


def shards(integrals, screen, coefficients, weights):
    aux_count = integrals.shape[0]
    row_count = integrals.shape[1]
    basis_count = integrals.shape[2]
    occ_count = coefficients.shape[1]
    row_blocks = row_count // BLOCK
    col_blocks = basis_count // BLOCK
    masks = screen.reshape(aux_count, row_blocks, 1, col_blocks, 1).astype(jnp.bfloat16)
    masked = integrals.reshape(aux_count, row_blocks, BLOCK, col_blocks, BLOCK) * masks
    flat = masked.reshape(aux_count * row_count, basis_count)
    summed_half = jnp.dot(
        flat,
        lax.all_gather(coefficients, "bas", axis=0, tiled=True),
        preferred_element_type=jnp.float32,
    )
    half = summed_half.reshape(aux_count, row_count, occ_count).transpose(1, 0, 2)
    half = half.reshape(row_count, aux_count * occ_count).astype(jnp.bfloat16)
    aux_groups = lax.axis_size("aux")
    scale = 1.0 / math.sqrt(AUX_DEV * aux_groups * NOCC)
    every = lax.all_gather(half, "aux", axis=1, tiled=True)
    weighted_all = (every.astype(jnp.float32) * jnp.tile(weights, aux_count * aux_groups)).astype(
        jnp.bfloat16
    )
    spread = lax.axis_size("bas") // aux_groups
    first = lax.axis_index("aux") * spread
    received = [spread_2(every, "bas", first + offset) for offset in range(spread)]
    owned = jnp.concatenate(received, axis=0)
    per_group = aux_count * occ_count
    left = owned.reshape(owned.shape[0], aux_groups, per_group)
    right = weighted_all.reshape(row_count, aux_groups, per_group)
    terms = jnp.einsum("ngk,mgk->gnm", left, right, preferred_element_type=jnp.float32)
    rounded = lax.optimization_barrier(terms.astype(jnp.bfloat16))
    total = jnp.sum(rounded.astype(jnp.float32), axis=0)
    return (total * scale).astype(jnp.bfloat16)


def solution(mesh):
    in_specs = (P("aux", "bas", None), P("aux", "bas", None), P("bas", None), P())
    out_specs = P("aux", "bas")
    return jax.shard_map(shards, mesh=mesh, in_specs=in_specs, out_specs=out_specs, check_vma=False)
```

profile of v0, /device:TPU:0, one launch (start us, length us, event | category | flops | bytes accessed | tf_op | source)
XLA Modules:
  0.0 303.1 jit_solution(3715893133542091083)
XLA Ops:
  6.5 0.0 all-gather.3.cloned.1.call-start
  6.5 0.7 all-gather.3.cloned.1.call-update
  7.3 0.0 all-gather.5.cloned.1.call-start
  7.3 0.7 convert_bitcast_fusion
  8.0 49.4 %all-gather.3.cloned.1.call-done = bf16[8192,384]{1,0:T(8,128)(2,1)} async-done(((bf16[1024,384]{1,0:T(8,128)(2,1)}), bf16[8192,384]{1,0:T(8,128)(2,1)}) %all-gather.3.cloned.1.call-update) | async-done | bytes 6291472 | tf_op jit(solution)/shard_map/all_gather | solution.py:29
  57.4 6.5 %mul.33 = bf16[8,128,64,128]{3,2,1,0:T(8,128)(2,1)} broadcast(bf16[8,64]{1,0:T(8,128)(2,1)S(1)} %convert_bitcast_fusion), dimensions={0,2} | broadcast | bytes 16778240 | tf_op jit(solution)/shard_map/mul | solution.py:25
  63.8 26.9 %fusion.7 = bf16[1024,384]{1,0:T(8,128)(2,1)} fusion(bf16[8192,384]{1,0:T(8,128)(2,1)} %all-gather.3.cloned.1.call-done, bf16[128,8,64,128]{3,2,1,0:T(8,128)(2,1)} %bitcast.25, bf16[1,1024,8192]{2,1,0:T(8,128)(2,1)} %param.4), kind=kOutput, calls=%fused_computation.15 | convolution fusion | flops 6451232768 | bytes 40632320 | tf_op jit(solution)/shard_map/dot_general | solution.py:27
  90.7 0.0 all-gather.5.cloned.1.call-update
  90.7 0.2 all-reduce.3.cloned.1.call-start
  90.9 0.0 copy-start.2
  91.0 63.1 %all-gather.5.cloned.1.call-done = bf16[1024,1536]{1,0:T(8,128)(2,1)} async-done(((bf16[1024,384]{1,0:T(8,128)(2,1)}), bf16[1024,1536]{1,0:T(8,128)(2,1)}) %all-gather.5.cloned.1.call-update) | async-done | bytes 3145744 | tf_op jit(solution)/shard_map/all_gather | solution.py:36
  154.1 0.0 copy-start
  154.1 5.2 %broadcast_select_fusion.1 = (bf16[1024,1536]{1,0:T(8,128)(2,1)}, bf16[1024,1536]{1,0:T(8,128)(2,1)}) fusion(bf16[1024,1536]{1,0:T(8,128)(2,1)} %all-gather.5.cloned.1.call-done, pred[]{:T(512)S(6)} %eq.6, pred[]{:T(512)S(6)} %eq.7), kind=kLoop, calls=%fused_computation.14 | loop fusion | flops 3145728 | bytes 9437186 | tf_op jit(solution)/shard_map/jit(_where)/select_n | solution.py:13
  159.3 0.0 all-reduce.3.cloned.1.call-update
  159.3 0.0 copy-done.2
  159.3 0.0 copy-done
  159.3 2.3 multiply_convert_fusion.1
  161.6 100.4 %all-reduce.3.cloned.1.call-done = (bf16[1024,1536]{1,0:T(8,128)(2,1)}, bf16[1024,1536]{1,0:T(8,128)(2,1)}) async-done(((bf16[1024,1536]{1,0:T(8,128)(2,1)}, bf16[1024,1536]{1,0:T(8,128)(2,1)}), (bf16[1024,1536]{1,0:T(8,128)(2,1)}, bf16[1024,1536]{1,0:T(8,128)(2,1)})) %all-reduce.3.cloned.1.call-update) | async-done | bytes 6291472 | tf_op jit(solution)/shard_map/psum | solution.py:14
  262.0 0.0 copy-start.1
  262.0 6.1 %pad_maximum_fusion = bf16[2048,1536]{1,0:T(8,128)(2,1)} fusion(bf16[1024,1536]{1,0:T(8,128)(2,1)} %get-tuple-element.5, bf16[1024,1536]{1,0:T(8,128)(2,1)} %get-tuple-element.6), kind=kLoop, calls=%fused_computation.9 | loop fusion | flops 12582912 | bytes 12582912 | tf_op jit(solution)/shard_map/concatenate | solution.py:43
  268.0 0.0 copy-done.1
  268.0 15.3 %convolution_convert_fusion = bf16[4,2048,1024]{2,1,0:T(8,128)(2,1)} fusion(bf16[256,4,8,384]{3,2,1,0:T(8,128)(2,1)} %bitcast.26, bf16[128,4,8,384]{3,2,1,0:T(8,128)(2,1)S(1)} %bitcast.27), kind=kOutput, calls=%fused_computation.5 | convolution fusion | flops 6450839552 | bytes 26214400 | tf_op jit(solution)/shard_map/ngk,mgk->gnm/dot_general | solution.py:47
  283.3 9.8 %convert_reduce_fusion = f32[2048,1024]{1,0:T(8,128)S(1)} fusion(bf16[4,2048,1024]{2,1,0:T(8,128)(2,1)} %convolution_convert_fusion), kind=kLoop, calls=%fused_computation | loop fusion | flops 14680064 | bytes 25165824 | tf_op jit(solution)/shard_map/reduce_sum | solution.py:49
  293.2 3.4 %multiply_convert_fusion = bf16[2048,1024]{1,0:T(8,128)(2,1)} fusion(f32[2048,1024]{1,0:T(8,128)S(1)} %convert_reduce_fusion), kind=kLoop, calls=%fused_computation.6 | loop fusion | flops 4194304 | bytes 12582912 | tf_op jit(solution)/shard_map/convert_element_type | solution.py:50
  (2 shorter events, 0.0 us)
Async XLA Ops:
  6.5 50.8 %all-gather.3.cloned.1.call-start = ((), (), s32[]{:S(2)}) async-start(), calls=%async_computation | async-start | bytes 7077888 | tf_op jit(solution)/shard_map/all_gather | solution.py:29
  7.3 146.8 %all-gather.5.cloned.1.call-start = ((), (), s32[]{:S(2)}) async-start(), calls=%async_computation.1 | async-start | bytes 3932160 | tf_op jit(solution)/shard_map/all_gather | solution.py:36
  90.7 171.3 %all-reduce.3.cloned.1.call-start = ((), (), s32[]{:S(2)}) async-start(), calls=%async_computation.2 | async-start | bytes 12582912 | tf_op jit(solution)/shard_map/psum | solution.py:14
  90.9 68.3 %copy-start.2 = (f32[384]{0:T(512)S(1)}, f32[384]{0:T(512)}, u32[]{:S(2)}) copy-start(f32[384]{0:T(512)} %param.7) | copy-start | bytes 4612
  154.1 5.2 %copy-start = (bf16[1024,1536]{1,0:T(8,128)(2,1)S(1)}, bf16[1024,1536]{1,0:T(8,128)(2,1)}, u32[]{:S(2)}) copy-start(bf16[1024,1536]{1,0:T(8,128)(2,1)} %all-gather.5.cloned.1.call-done) | copy-start | bytes 9437188
  262.0 6.1 %copy-start.1 = (bf16[1024,1536]{1,0:T(8,128)(2,1)S(1)}, bf16[1024,1536]{1,0:T(8,128)(2,1)}, u32[]{:S(2)}) copy-start(bf16[1024,1536]{1,0:T(8,128)(2,1)} %multiply_convert_fusion.1) | copy-start | bytes 9437188
Sparse Core Ops, SparseCore 0:
  9.2 48.1 all-gather.2
  90.8 63.2 all-gather.4
  159.4 102.5 all-reduce.2
where the time goes:
time: 303 us
  waiting for transfers between devices  214 us (71%)
  matrix products  42.1 us (14%)
  other arithmetic  27.4 us (9%)
  between operations  13.2 us (4%)
  local copies, waits for them, and re-layouts  6.49 us (2%)
    psum x1, waiting for transfers between devices, spread_2(): return lax.psum(block, axis)  100 us
    all_gather x1, waiting for transfers between devices, shards(): every = lax.all_gather(half, 'aux', axis=1, tiled=True)  63.1 us
    all_gather x1, waiting for transfers between devices, shards(): lax.all_gather(coefficients, 'bas', axis=0, tiled=True)  49.4 us
    dot_general x1, matrix products, shards(): jnp.dot(flat, lax.all_gather(coefficients, 'bas', axis=0, tiled=True), pr...  26.9 us
    dot_general x1, matrix products, shards(): jnp.einsum('ngk,mgk->gnm', left, right, preferred_element_type=jnp.float32)  15.3 us
    reduce_sum x1, other arithmetic, shards(): total = jnp.sum(rounded.astype(jnp.float32), axis=0)  9.83 us
    mul x1, local copies, waits for them, and re-layouts, shards(): integrals.reshape(aux_count, row_blocks, BLOCK, col_blocks, BLOCK) * masks  6.46 us
  transfers between devices with their start and end apart: 3, of which 3 were waited for; matrix products, arithmetic and copies ran while one was open for 1% of the time, Pallas kernels for 0%

commit v1 on v0

--- a/solution.py
+++ b/solution.py
@@ -33,7 +33,12 @@
     half = half.reshape(row_count, aux_count * occ_count).astype(jnp.bfloat16)
     aux_groups = lax.axis_size("aux")
     scale = 1.0 / math.sqrt(AUX_DEV * aux_groups * NOCC)
-    every = lax.all_gather(half, "aux", axis=1, tiled=True)
+    ring = [half]
+    for hop in range(3):
+        ring.append(lax.ppermute(ring[-1], "aux", [(dev, (dev + 1) % 4) for dev in range(4)]))
+    every = jnp.roll(
+        jnp.concatenate(ring[::-1], axis=1), (lax.axis_index("aux") + 1) * ring[0].shape[1], axis=1
+    )
     weighted_all = (every.astype(jnp.float32) * jnp.tile(weights, aux_count * aux_groups)).astype(
         jnp.bfloat16
     )

time: 303 us -> 287 us (0.947)
  matrix products: 42.1 us -> 28.2 us
  waiting for transfers between devices: 214 us -> 207 us
  local copies, waits for them, and re-layouts: 6.49 us -> 10.3 us
    all_gather x1 -> x0, waiting for transfers between devices: 63.1 us -> none  [shards(): every = lax.all_gather(half, 'aux', axis=1, tiled=True)]
    ppermute x0 -> x3, waiting for transfers between devices: none -> 60.4 us  [shards(): lax.ppermute(ring[-1], 'aux', [(dev, (dev + 1) % 4) for dev in range(4)])]
    dot_general x1, matrix products: 26.9 us -> 13.9 us  [shards(): jnp.dot(flat, lax.all_gather(coefficients, 'bas', axis=0, tiled=True), pr...]
    psum x1, waiting for transfers between devices: 100 us -> 96.8 us  [spread_2(): return lax.psum(block, axis)]
  transfers between devices with their start and end apart: 3 -> 5, of which waited for: 3 -> 5; matrix products, arithmetic and copies ran while one was open for 1% -> 2% of each run, Pallas kernels for 0% -> 0%
where the time goes in v1:
time: 287 us
  waiting for transfers between devices  207 us (72%)
  matrix products  28.2 us (10%)
  other arithmetic  26 us (9%)
  between operations  13.5 us (5%)
  local copies, waits for them, and re-layouts  10.3 us (4%)
    psum x1, waiting for transfers between devices, spread_2(): return lax.psum(block, axis)  96.8 us
    ppermute x3, waiting for transfers between devices, shards(): lax.ppermute(ring[-1], 'aux', [(dev, (dev + 1) % 4) for dev in range(4)])  60.4 us
    all_gather x1, waiting for transfers between devices, shards(): lax.all_gather(coefficients, 'bas', axis=0, tiled=True)  49.4 us
    dot_general x1, matrix products, shards(): jnp.einsum('ngk,mgk->gnm', left, right, preferred_element_type=jnp.float32)  14.3 us
    dot_general x1, matrix products, shards(): jnp.dot(flat, lax.all_gather(coefficients, 'bas', axis=0, tiled=True), pr...  13.9 us
    reduce_sum x1, other arithmetic, shards(): total = jnp.sum(rounded.astype(jnp.float32), axis=0)  9.83 us
    mul x1, local copies, waits for them, and re-layouts, shards(): integrals.reshape(aux_count, row_blocks, BLOCK, col_blocks, BLOCK) * masks  7.25 us
  transfers between devices with their start and end apart: 5, of which 5 were waited for; matrix products, arithmetic and copies ran while one was open for 2% of the time, Pallas kernels for 0%

profile of v1, /device:TPU:0, one launch (start us, length us, event | category | flops | bytes accessed | tf_op | source)
XLA Modules:
  0.0 287.0 jit_solution(6781122564902658973)
XLA Ops:
  6.5 0.0 all-gather.2.cloned.1.call-start
  6.5 0.7 all-gather.2.cloned.1.call-update
  7.3 0.0 all-reduce.3.cloned.1.call-start
  7.3 0.7 convert_bitcast_fusion
  8.0 49.4 %all-gather.2.cloned.1.call-done = bf16[8192,384]{1,0:T(8,128)(2,1)} async-done(((bf16[1024,384]{1,0:T(8,128)(2,1)}), bf16[8192,384]{1,0:T(8,128)(2,1)}) %all-gather.2.cloned.1.call-update) | async-done | bytes 6291472 | tf_op jit(solution)/shard_map/all_gather | solution.py:29
  57.4 7.2 %mul.36 = bf16[8,128,64,128]{3,2,1,0:T(8,128)(2,1)} broadcast(bf16[8,64]{1,0:T(8,128)(2,1)S(1)} %convert_bitcast_fusion), dimensions={0,2} | broadcast | bytes 16778240 | tf_op jit(solution)/shard_map/mul | solution.py:25
  64.6 0.0 copy-done.2
  64.6 13.9 %fusion.3 = bf16[1024,384]{0,1:T(8,128)(2,1)S(1)} fusion(bf16[8192,384]{1,0:T(8,128)(2,1)S(1)} %copy-done.2, bf16[128,8,64,128]{3,2,1,0:T(8,128)(2,1)} %bitcast.21, bf16[1,1024,8192]{2,1,0:T(8,128)(2,1)} %param.4), kind=kOutput, calls=%fused_computation.11 | convolution fusion | flops 6451232768 | bytes 40632320 | tf_op jit(solution)/shard_map/dot_general | solution.py:27
  78.6 1.5 collective-permute-start
  80.1 20.0 %collective-permute-done = bf16[1024,384]{0,1:T(8,128)(2,1)S(1)} collective-permute-done((bf16[1024,384]{0,1:T(8,128)(2,1)S(1)}, bf16[1024,384]{0,1:T(8,128)(2,1)S(1)}, u32[]{:S(2)}, u32[]{:S(2)}) %collective-permute-start) | collective-permute-done | bytes 786464 | tf_op jit(solution)/shard_map/ppermute | solution.py:38
  100.1 0.0 collective-permute-start.1
  100.1 20.6 %collective-permute-done.1 = bf16[1024,384]{0,1:T(8,128)(2,1)S(1)} collective-permute-done((bf16[1024,384]{0,1:T(8,128)(2,1)S(1)}, bf16[1024,384]{0,1:T(8,128)(2,1)S(1)}, u32[]{:S(2)}, u32[]{:S(2)}) %collective-permute-start.1) | collective-permute-done | bytes 786464 | tf_op jit(solution)/shard_map/ppermute | solution.py:38
  120.7 0.0 collective-permute-start.2
  120.7 19.8 %collective-permute-done.2 = bf16[1024,384]{0,1:T(8,128)(2,1)S(1)} collective-permute-done((bf16[1024,384]{0,1:T(8,128)(2,1)S(1)}, bf16[1024,384]{0,1:T(8,128)(2,1)S(1)}, u32[]{:S(2)}, u32[]{:S(2)}) %collective-permute-start.2) | collective-permute-done | bytes 786464 | tf_op jit(solution)/shard_map/ppermute | solution.py:38
  140.5 0.1 constant_dynamic-update-slice_fusion.7
  140.6 0.1 constant_dynamic-update-slice_fusion.6
  140.6 0.1 constant_dynamic-update-slice_fusion.5
  140.7 0.1 constant_dynamic-update-slice_fusion.4
  140.7 0.1 constant_dynamic-update-slice_fusion.3
  140.8 0.1 constant_dynamic-update-slice_fusion.2
  140.9 0.1 constant_dynamic-update-slice_fusion.1
  140.9 0.1 constant_dynamic-update-slice_fusion
  141.0 0.0 copy-start
  141.0 2.7 copy-done
  143.7 4.2 %broadcast_select_fusion.1 = (bf16[1024,1536]{0,1:T(8,128)(2,1)}, bf16[1024,1536]{0,1:T(8,128)(2,1)}) fusion(pred[]{:T(512)S(6)} %eq.9, bf16[1024,3072]{0,1:T(8,128)(2,1)S(1)} %constant_dynamic-update-slice_fusion, s32[]{:T(128)S(6)} %select_n.29, pred[]{:T(512)S(6)} %eq.10), kind=kLoop, calls=%fused_computation.10 | loop fusion | flops 3145728 | bytes 9437190 | tf_op jit(solution)/shard_map/jit(_where)/select_n | solution.py:13
  147.8 0.0 all-reduce.3.cloned.1.call-update
  147.9 4.5 %multiply_convert_fusion.1 = bf16[1024,1536]{0,1:T(8,128)(2,1)} fusion(f32[1536]{0:T(1024)S(1)} %mul.40, bf16[1024,3072]{0,1:T(8,128)(2,1)} %copy-done, s32[]{:T(128)S(6)} %select_n.29), kind=kLoop, calls=%fused_computation.8 | loop fusion | flops 4718592 | bytes 6297604 | tf_op jit(solution)/shard_map/convert_element_type | solution.py:42
  152.4 96.8 %all-reduce.3.cloned.1.call-done = (bf16[1024,1536]{0,1:T(8,128)(2,1)}, bf16[1024,1536]{0,1:T(8,128)(2,1)}) async-done(((bf16[1024,1536]{0,1:T(8,128)(2,1)}, bf16[1024,1536]{0,1:T(8,128)(2,1)}), (bf16[1024,1536]{0,1:T(8,128)(2,1)}, bf16[1024,1536]{0,1:T(8,128)(2,1)})) %all-reduce.3.cloned.1.call-update) | async-done | bytes 6291472 | tf_op jit(solution)/shard_map/psum | solution.py:14
  249.2 3.4 %pad_maximum_fusion = bf16[2048,1536]{0,1:T(8,128)(2,1)S(1)} fusion(bf16[1024,1536]{0,1:T(8,128)(2,1)} %get-tuple-element.5, bf16[1024,1536]{0,1:T(8,128)(2,1)} %get-tuple-element.6), kind=kLoop, calls=%fused_computation.7 | loop fusion | flops 12582912 | bytes 12582912 | tf_op jit(solution)/shard_map/concatenate | solution.py:48
  252.6 14.3 %convolution_convert_fusion = bf16[4,2048,1024]{2,1,0:T(8,128)(2,1)} fusion(bf16[2048,4,384]{0,2,1:T(8,128)(2,1)S(1)} %bitcast.22, bf16[1024,4,384]{0,2,1:T(8,128)(2,1)} %bitcast.23), kind=kOutput, calls=%fused_computation.5 | convolution fusion | flops 6450839552 | bytes 26214400 | tf_op jit(solution)/shard_map/ngk,mgk->gnm/dot_general | solution.py:52
  266.9 9.8 %convert_reduce_fusion = f32[2048,1024]{1,0:T(8,128)S(1)} fusion(bf16[4,2048,1024]{2,1,0:T(8,128)(2,1)} %convolution_convert_fusion), kind=kLoop, calls=%fused_computation | loop fusion | flops 14680064 | bytes 25165824 | tf_op jit(solution)/shard_map/reduce_sum | solution.py:54
  276.8 3.4 %multiply_convert_fusion = bf16[2048,1024]{1,0:T(8,128)(2,1)} fusion(f32[2048,1024]{1,0:T(8,128)S(1)} %convert_reduce_fusion), kind=kLoop, calls=%fused_computation.6 | loop fusion | flops 4194304 | bytes 12582912 | tf_op jit(solution)/shard_map/convert_element_type | solution.py:55
  (5 shorter events, 0.0 us)
Async XLA Ops:
  6.5 50.8 %all-gather.2.cloned.1.call-start = ((), (), s32[]{:S(2)}) async-start(), calls=%async_computation | async-start | bytes 7077888 | tf_op jit(solution)/shard_map/all_gather | solution.py:29
  7.3 241.9 %all-reduce.3.cloned.1.call-start = ((), (), s32[]{:S(2)}) async-start(), calls=%async_computation.1 | async-start | bytes 12582912 | tf_op jit(solution)/shard_map/psum | solution.py:14
  57.4 7.3 %copy-start.2 = (bf16[8192,384]{1,0:T(8,128)(2,1)S(1)}, bf16[8192,384]{1,0:T(8,128)(2,1)}, u32[]{:S(2)}) copy-start(bf16[8192,384]{1,0:T(8,128)(2,1)} %all-gather.2.cloned.1.call-done) | copy-start | bytes 18874372
  78.6 21.5 %collective-permute-start = (bf16[1024,384]{0,1:T(8,128)(2,1)S(1)}, bf16[1024,384]{0,1:T(8,128)(2,1)S(1)}, u32[]{:S(2)}, u32[]{:S(2)}) collective-permute-start(bf16[1024,384]{0,1:T(8,128)(2,1)S(1)} %fusion.3), channel_id=1, source_target_pairs={{0,1},{1,2},{2,3},{3,0},{4,5},{5,6},{6,7},{7,4},{8,9},{9,10},{10,1... | collective-permute-start | bytes 2359304 | tf_op jit(solution)/shard_map/ppermute | solution.py:38
  100.1 20.6 %collective-permute-start.1 = (bf16[1024,384]{0,1:T(8,128)(2,1)S(1)}, bf16[1024,384]{0,1:T(8,128)(2,1)S(1)}, u32[]{:S(2)}, u32[]{:S(2)}) collective-permute-start(bf16[1024,384]{0,1:T(8,128)(2,1)S(1)} %collective-permute-done), channel_id=1, source_target_pairs={{0,1},{1,2},{2,3},{3,0},{4,5},{5,6},{6,7},{7,4},{8,9},{9,10},{10,1... | collective-permute-start | bytes 2359304 | tf_op jit(solution)/shard_map/ppermute | solution.py:38
  120.7 19.8 %collective-permute-start.2 = (bf16[1024,384]{0,1:T(8,128)(2,1)S(1)}, bf16[1024,384]{0,1:T(8,128)(2,1)S(1)}, u32[]{:S(2)}, u32[]{:S(2)}) collective-permute-start(bf16[1024,384]{0,1:T(8,128)(2,1)S(1)} %collective-permute-done.1), channel_id=1, source_target_pairs={{0,1},{1,2},{2,3},{3,0},{4,5},{5,6},{6,7},{7,4},{8,9},{9,10},{10,1... | collective-permute-start | bytes 2359304 | tf_op jit(solution)/shard_map/ppermute | solution.py:38
  141.0 2.7 copy-start
  143.7 4.2 %copy-start.1 = (f32[384]{0:T(512)S(1)}, f32[384]{0:T(512)}, u32[]{:S(2)}) copy-start(f32[384]{0:T(512)} %param.7) | copy-start | bytes 4612
Sparse Core Ops, SparseCore 0:
  9.2 48.1 all-gather.1
  148.0 101.1 all-reduce.2
